TPU v7x, 512 devices: a whole 4x4x16 slice. The times are simulated.
512 devices in a mesh: gz: 128 (over z, y, core), row: 4 (over x).
Axes of the slice: x: 4, y: 4, z: 16, core: 2. Of those that a mesh axis runs over, the one named last changes fastest.
Arguments:
- tokens: bfloat16 [262144, 384], P(('gz', 'row')), may hold values from -6 to 6
- key_blocks: int32 [4096, 20], P(('gz', 'row')), may hold values from 0 to 4095, as said below
- counts: int32 [128], replicated, may hold values from 8 to 32, as said below
- norm_gain: float32 [384], replicated, may hold values from 0.1 to 1.9
- qkv_weight: bfloat16 [384, 1152], replicated, may hold values from -1 to 1
- out_weight: bfloat16 [384, 384], replicated, may hold values from -0.3125 to 0.3125
- mlp_gain: float32 [384], replicated, may hold values from 0.1 to 1.9
- up_weight: bfloat16 [384, 1536], replicated, may hold values from -0.3125 to 0.3125
- down_weight: bfloat16 [1536, 384], replicated, may hold values from -0.15625 to 0.15625
Outputs:
- block_out: bfloat16 [262144, 384], P(('gz', 'row'))
Inputs may be any that keep to these rules, and one draw needn't show every extreme that they name: `key_blocks`: entries 0 to 3 of a query block's list name live blocks of the query's own slab (repeats possible). The other 16 entries name blocks with the same row group as the query block (id % 32 // 8 equal), in any slab; over the blocks of one device each slab is named by exactly 1 such entries. `counts`: one slab is full in every draw.
All inputs are finite; a program needn't handle non-finite values.
Results may differ from a plain program's by a relative error of at most 0.01.
Values may be sent and summed in bfloat16 or wider, within the bound.
A program may use at most 128 MiB of HBM per device.

v0:
```python
import jax
import jax.numpy as jnp
from jax import lax
from jax.sharding import PartitionSpec as P

H = 12
NNEAR = 4
NFAR = 16


def rms_norm(values, gain):
    mean_sq = jnp.mean(values * values, axis=-1, keepdims=True)
    return values * lax.rsqrt(mean_sq + 1e-05) * gain


def attend(query_block, key_values, live_blocks):
    model_width = query_block.shape[1]
    head_size = model_width // H
    keys = key_values[:, :, :model_width].reshape(-1, H, head_size)
    values = key_values[:, :, model_width:].reshape(-1, H, head_size)
    heads = query_block.reshape(-1, H, head_size)
    scores = jnp.einsum("qhd,khd->hqk", heads, keys, preferred_element_type=jnp.float32) / jnp.sqrt(
        jnp.float32(head_size)
    )
    key_live = jnp.repeat(live_blocks, key_values.shape[1])
    scores = jnp.where(key_live[None, None, :], scores, jnp.float32(-1e30))
    top = jnp.max(scores, axis=-1, keepdims=True)
    weights = jnp.exp(scores - top)
    total = jnp.sum(weights, axis=-1)
    mixed = jnp.einsum(
        "hqk,khd->qhd", weights.astype(jnp.bfloat16), values, preferred_element_type=jnp.float32
    )
    mixed = mixed / jnp.transpose(total)[:, :, None]
    return mixed.reshape(-1, model_width).astype(jnp.bfloat16)


def body(
    tokens, key_blocks, counts, norm_gain, qkv_weight, out_weight, mlp_gain, up_weight, down_weight
):
    model_width = tokens.shape[1]
    own_blocks = key_blocks.shape[0]
    block_len = tokens.shape[0] // own_blocks
    slabs_n = lax.axis_size("gz")
    slab_blocks = own_blocks * lax.axis_size("row")
    inputs = tokens.astype(jnp.float32)
    normed = rms_norm(inputs, norm_gain).astype(jnp.bfloat16)
    projected = jnp.dot(normed, qkv_weight, preferred_element_type=jnp.float32).astype(jnp.bfloat16)
    queries = projected[:, :model_width].reshape(own_blocks, block_len, model_width)
    kv_own = projected[:, model_width:].reshape(own_blocks, block_len, 2 * model_width)
    slab_kv = lax.all_gather(kv_own, "row", axis=0, tiled=True)
    owner_slab = key_blocks // slab_blocks
    within = key_blocks % slab_blocks
    slab_table = jnp.arange(slabs_n, dtype=jnp.int32)
    slab_count = jnp.sum(jnp.where(owner_slab[:, :, None] == slab_table, counts, 0), axis=-1)
    live = within < slab_count
    near_rows = within[:, :NNEAR]
    far_owner = owner_slab[:, NNEAR:].reshape(-1)
    far_local = (key_blocks[:, NNEAR:] % own_blocks).reshape(-1)
    request_count = far_owner.shape[0]
    per_owner = request_count // slabs_n
    slab_hits = (far_owner[:, None] == slab_table[None, :]).astype(jnp.int32)
    slot_rank = jnp.sum((jnp.cumsum(slab_hits, axis=0) - 1) * slab_hits, axis=1)
    far_slot = far_owner * per_owner + slot_rank
    slot_hits = far_slot[:, None] == jnp.arange(request_count, dtype=jnp.int32)[None, :]
    request = jnp.sum(jnp.where(slot_hits, far_local[:, None], 0), axis=0)
    wanted = lax.all_to_all(
        request.reshape(slabs_n, per_owner), "gz", split_axis=0, concat_axis=0, tiled=True
    ).reshape(-1)
    kv_sent = kv_own[wanted].reshape(slabs_n, per_owner, block_len, 2 * model_width)
    far_kv = lax.all_to_all(kv_sent, "gz", split_axis=0, concat_axis=0, tiled=True).reshape(
        request_count, block_len, 2 * model_width
    )
    far_slots = far_slot.reshape(own_blocks, NFAR)

    def one_block(packed):
        query_block, near_row, slot_row, live_blocks = packed
        gathered = jnp.concatenate([slab_kv[near_row], far_kv[slot_row]], axis=0)
        return attend(query_block, gathered, live_blocks)

    attended = lax.map(one_block, (queries, near_rows, far_slots, live)).reshape(-1, model_width)
    residual = (inputs + jnp.dot(attended, out_weight, preferred_element_type=jnp.float32)).astype(
        jnp.bfloat16
    )
    normed_two = rms_norm(residual.astype(jnp.float32), mlp_gain).astype(jnp.bfloat16)
    hidden = jax.nn.gelu(jnp.dot(normed_two, up_weight, preferred_element_type=jnp.float32)).astype(
        jnp.bfloat16
    )
    result = residual.astype(jnp.float32) + jnp.dot(
        hidden, down_weight, preferred_element_type=jnp.float32
    )
    return result.astype(jnp.bfloat16)


def solution(mesh):
    return jax.shard_map(
        body,
        mesh=mesh,
        in_specs=(
            P(("gz", "row"), None),
            P(("gz", "row"), None),
            P(),
            P(),
            P(),
            P(),
            P(),
            P(),
            P(),
        ),
        out_specs=P(("gz", "row"), None),
        check_vma=False,
    )
```

profile of v0, /device:TPU:34, one launch (start us, length us, event | category | flops | bytes accessed | tf_op | source)
XLA Modules:
  0.0 899.9 jit_solution(1121670228715320951)
XLA Ops:
  9.8 19.2 %all-to-all-start = ((s32[128,1,1]{2,1,0:T(1,128)}), s32[128,1,1]{2,1,0:T(1,128)S(1)}, u32[]{:S(2)}, u32[]{:S(2)}) async-start(s32[128,1,1]{2,1,0:T(1,128)} %copy.50), calls=%async_computation | async-start | bytes 131072 | tf_op jit(solution)/shard_map/all_to_all | solution.py:66
  33.1 10.2 %all-to-all-done = s32[128,1,1]{2,1,0:T(1,128)S(1)} async-done(((s32[128,1,1]{2,1,0:T(1,128)}), s32[128,1,1]{2,1,0:T(1,128)S(1)}, u32[]{:S(2)}, u32[]{:S(2)}) %all-to-all-start) | async-done | bytes 544 | tf_op jit(solution)/shard_map/all_to_all | solution.py:66
  45.6 8.3 gather_fusion.2
  53.9 7.6 all-to-all-start.1
  65.7 46.3 %all-gather.2.cloned.1.call-done = bf16[32,64,768]{2,1,0:T(8,128)(2,1)} async-done(((bf16[8,64,768]{2,1,0:T(8,128)(2,1)}), bf16[32,64,768]{2,1,0:T(8,128)(2,1)}) %all-gather.2.cloned.1.call-update) | async-done | bytes 3145744 | tf_op jit(solution)/shard_map/all_gather | solution.py:50
  112.0 496.7 %all-to-all-done.1 = bf16[128,1,64,768]{3,2,1,0:T(8,128)(2,1)} async-done(((bf16[128,1,64,768]{3,2,1,0:T(8,128)(2,1)}), bf16[128,1,64,768]{3,2,1,0:T(8,128)(2,1)}, u32[]{:S(2)}, u32[]{:S(2)}) %all-to-all-start.1) | async-done | bytes 12582944 | tf_op jit(solution)/shard_map/all_to_all | solution.py:70
  608.7 278.2 %while.10 = (s32[]{:T(128)}, bf16[8,64,384]{2,1,0:T(8,128)(2,1)}, s32[8,4]{1,0:T(8,128)}, bf16[32,64,768]{2,1,0:T(8,128)(2,1)}, s32[8,16]{1,0:T(8,128)}, /*index...) while((s32[]{:T(128)}, bf16[8,64,384]{2,1,0:T(8,128)(2,1)}, ...), condition=%wide.region_8.9_spmd, body=%wide.region_5.8_spmd.sunk | while | flops 132760128 | bytes 49673220 | solution.py:80
  613.4 5.2 gather_fusion.1
  639.6 3.1 fusion.79
  648.1 5.2 gather_fusion.1
  674.4 3.1 fusion.79
  682.9 5.2 gather_fusion.1
  709.2 3.1 fusion.79
  717.7 5.2 gather_fusion.1
  743.9 3.1 fusion.79
  752.5 5.2 gather_fusion.1
  778.7 3.1 fusion.79
  787.2 5.2 gather_fusion.1
  813.5 3.1 fusion.79
  822.0 5.2 gather_fusion.1
  848.3 3.1 fusion.79
  856.8 5.2 gather_fusion.1
  883.0 3.1 fusion.79
  888.6 3.5 fusion.29
  (221 shorter events, 227.2 us)
Async XLA Ops:
  6.5 882.0 %copy-start = (bf16[1536,384]{1,0:T(8,128)(2,1)S(1)}, bf16[1536,384]{1,0:T(8,128)(2,1)}, u32[]{:S(2)}) copy-start(bf16[1536,384]{1,0:T(8,128)(2,1)} %param.19) | copy-start | bytes 3538948
  9.8 33.5 %all-to-all-start = ((s32[128,1,1]{2,1,0:T(1,128)}), s32[128,1,1]{2,1,0:T(1,128)S(1)}, u32[]{:S(2)}, u32[]{:S(2)}) async-start(s32[128,1,1]{2,1,0:T(1,128)} %copy.50), calls=%async_computation | async-start | bytes 131072 | tf_op jit(solution)/shard_map/all_to_all | solution.py:66
  30.1 0.8 copy-start.3
  33.1 20.9 %copy-start.2 = (bf16[512,768]{1,0:T(8,128)(2,1)}, bf16[512,768]{1,0:T(8,128)(2,1)S(1)}, u32[]{:S(2)}) copy-start(bf16[512,768]{1,0:T(8,128)(2,1)S(1)} %slice.35) | copy-start | bytes 2359300
  53.9 10.0 %copy-start.4 = (s32[128]{0:T(128)S(1)}, s32[128]{0:T(128)}, u32[]{:S(2)}) copy-start(s32[128]{0:T(128)} %param.13) | copy-start | bytes 1540
  53.9 554.8 %all-to-all-start.1 = ((bf16[128,1,64,768]{3,2,1,0:T(8,128)(2,1)}), bf16[128,1,64,768]{3,2,1,0:T(8,128)(2,1)}, u32[]{:S(2)}, u32[]{:S(2)}) async-start(bf16[128,1,64,768]{3,2,1,0:T(8,128)(2,1)} %bitcast.77), calls=%async_computation.1 | async-start | bytes 25165824 | tf_op jit(solution)/shard_map/all_to_all | solution.py:70
  61.5 50.5 %all-gather.2.cloned.1.call-start = ((), (), s32[]{:S(2)}) async-start(), calls=%async_computation.2 | async-start | bytes 3932160 | tf_op jit(solution)/shard_map/all_gather | solution.py:50
  631.8 1.9 copy-start.1
  666.6 1.9 copy-start.1
  701.4 1.9 copy-start.1
  736.2 1.9 copy-start.1
  770.9 1.9 copy-start.1
  805.7 1.9 copy-start.1
  840.5 1.9 copy-start.1
  875.3 1.9 copy-start.1
Sparse Core Ops, SparseCore 0:
  64.5 47.5 all-gather.1
where the time goes:
time: 903 us; the launch traced here: 900 us
  waiting for transfers between devices  554 us (61%)
  local copies, waits for them, and re-layouts  236 us (26%)
  matrix products  48.5 us (5%)
  starting transfers between devices  27 us (3%)
  other arithmetic  21.2 us (2%)
  between operations  13.5 us (1%)
    all_to_all x1, waiting for transfers between devices, body(): lax.all_to_all(kv_sent, 'gz', split_axis=0, concat_axis=0, tiled=True)  497 us
    gather x16, local copies, waits for them, and re-layouts, one_block(): gathered = jnp.concatenate([slab_kv[near_row], far_kv[slot_row]], axis=0)  61.5 us
    all_gather x1, waiting for transfers between devices, body(): slab_kv = lax.all_gather(kv_own, 'row', axis=0, tiled=True)  46.3 us
    slice x16, local copies, waits for them, and re-layouts, attend(): keys = key_values[:, :, :model_width].reshape(-1, H, head_size)  46.1 us
    dot_general x8, matrix products, attend(): jnp.einsum('hqk,khd->qhd', weights.astype(jnp.bfloat16), values, preferre...  25.1 us
    slice x8, local copies, waits for them, and re-layouts, attend(): values = key_values[:, :, model_width:].reshape(-1, H, head_size)  22.3 us
    while x24, local copies, waits for them, and re-layouts  21.4 us
    all_to_all x1, starting transfers between devices, body(): lax.all_to_all(request.reshape(slabs_n, per_owner), 'gz', split_axis=0, c...  19.2 us
  transfers between devices with their start and end apart: 3, of which 3 were waited for; matrix products, arithmetic and copies ran while one was open for 1% of the time, Pallas kernels for 0%

commit v1 on v0

--- a/solution.py
+++ b/solution.py
@@ -47,7 +47,14 @@
     projected = jnp.dot(normed, qkv_weight, preferred_element_type=jnp.float32).astype(jnp.bfloat16)
     queries = projected[:, :model_width].reshape(own_blocks, block_len, model_width)
     kv_own = projected[:, model_width:].reshape(own_blocks, block_len, 2 * model_width)
-    slab_kv = lax.all_gather(kv_own, "row", axis=0, tiled=True)
+    n_dev = lax.axis_size("row")
+    right = [(i, (i + 1) % n_dev) for i in range(n_dev)]
+    pieces = [kv_own]
+    for hop in range(1, n_dev):
+        pieces = [lax.ppermute(pieces[0], "row", right), *pieces]
+    whole = jnp.concatenate(pieces, axis=0)
+    places = (lax.axis_index("row") + 1) * pieces[-1].shape[0]
+    slab_kv = jnp.roll(whole, places, axis=0)
     owner_slab = key_blocks // slab_blocks
     within = key_blocks % slab_blocks
     slab_table = jnp.arange(slabs_n, dtype=jnp.int32)

time: 903 us -> 855 us (0.947)
  waiting for transfers between devices: 554 us -> 530 us
  matrix products: 48.5 us -> 29.6 us
  between operations: 13.5 us -> 0.25 us
  starting transfers between devices: 27 us -> 37 us
    all_gather x1 -> x0, waiting for transfers between devices: 46.3 us -> none  [body(): slab_kv = lax.all_gather(kv_own, 'row', axis=0, tiled=True)]
    ppermute x0 -> x3, waiting for transfers between devices: none -> 41.6 us  [body(): pieces = [lax.ppermute(pieces[0], 'row', right), *pieces]]
    dot_general x8, matrix products: 25.1 us -> 5.77 us  [attend(): jnp.einsum('hqk,khd->qhd', weights.astype(jnp.bfloat16), values, preferre...]
    all_to_all x1, waiting for transfers between devices: 497 us -> 479 us  [body(): lax.all_to_all(kv_sent, 'gz', split_axis=0, concat_axis=0, tiled=True)]
    while x24, local copies, waits for them, and re-layouts: 21.4 us -> 10 us
    ppermute x0 -> x3, starting transfers between devices: none -> 10.4 us  [body(): pieces = [lax.ppermute(pieces[0], 'row', right), *pieces]]
  transfers between devices with their start and end apart: 3 -> 5, of which waited for: 3 -> 5; matrix products, arithmetic and copies ran while one was open for 1% -> 2% of each run, Pallas kernels for 0% -> 0%
where the time goes in v1:
time: 855 us; the launch traced here: 851 us
  waiting for transfers between devices  530 us (62%)
  local copies, waits for them, and re-layouts  234 us (27%)
  starting transfers between devices  37 us (4%)
  matrix products  29.6 us (3%)
  other arithmetic  19.8 us (2%)
    all_to_all x1, waiting for transfers between devices, body(): lax.all_to_all(kv_sent, 'gz', split_axis=0, concat_axis=0, tiled=True)  479 us
    gather x16, local copies, waits for them, and re-layouts, one_block(): gathered = jnp.concatenate([slab_kv[near_row], far_kv[slot_row]], axis=0)  61.4 us
    slice x16, local copies, waits for them, and re-layouts, attend(): keys = key_values[:, :, :model_width].reshape(-1, H, head_size)  46.2 us
    ppermute x3, waiting for transfers between devices, body(): pieces = [lax.ppermute(pieces[0], 'row', right), *pieces]  41.6 us
    slice x8, local copies, waits for them, and re-layouts, attend(): values = key_values[:, :, model_width:].reshape(-1, H, head_size)  22.3 us
    all_to_all x1, starting transfers between devices, body(): lax.all_to_all(request.reshape(slabs_n, per_owner), 'gz', split_axis=0, c...  19.2 us
    reshape x8, local copies, waits for them, and re-layouts, attend(): values = key_values[:, :, model_width:].reshape(-1, H, head_size)  19 us
    reshape x8, local copies, waits for them, and re-layouts, attend(): keys = key_values[:, :, :model_width].reshape(-1, H, head_size)  18.6 us
  transfers between devices with their start and end apart: 5, of which 5 were waited for; matrix products, arithmetic and copies ran while one was open for 2% of the time, Pallas kernels for 0%

profile of v1, /device:TPU:34, one launch (start us, length us, event | category | flops | bytes accessed | tf_op | source)
XLA Modules:
  0.0 850.8 jit_solution(8200928860401951791)
XLA Ops:
  3.8 19.2 %all-to-all-start = ((s32[128,1,1]{2,1,0:T(1,128)}), s32[128,1,1]{2,1,0:T(1,128)S(1)}, u32[]{:S(2)}, u32[]{:S(2)}) async-start(s32[128,1,1]{2,1,0:T(1,128)} %copy.48), calls=%async_computation | async-start | bytes 131072 | tf_op jit(solution)/shard_map/all_to_all | solution.py:73
  28.2 9.1 %all-to-all-done = s32[128,1,1]{2,1,0:T(1,128)S(1)} async-done(((s32[128,1,1]{2,1,0:T(1,128)}), s32[128,1,1]{2,1,0:T(1,128)S(1)}, u32[]{:S(2)}, u32[]{:S(2)}) %all-to-all-start) | async-done | bytes 544 | tf_op jit(solution)/shard_map/all_to_all | solution.py:73
  39.7 8.3 gather_fusion.2
  48.0 7.5 all-to-all-start.1
  55.5 3.4 collective-permute-start
  58.9 18.1 %collective-permute-done = bf16[8,64,768]{2,1,0:T(8,128)(2,1)S(1)} collective-permute-done((bf16[8,64,768]{2,1,0:T(8,128)(2,1)S(1)}, bf16[8,64,768]{2,1,0:T(8,128)(2,1)S(1)}, u32[]{:S(2)}, u32[]{:S(2)}) %collective-permute-start) | collective-permute-done | bytes 786464 | tf_op jit(solution)/shard_map/ppermute | solution.py:54
  76.9 3.4 collective-permute-start.1
  80.3 17.4 %collective-permute-done.1 = bf16[8,64,768]{2,1,0:T(8,128)(2,1)S(1)} collective-permute-done((bf16[8,64,768]{2,1,0:T(8,128)(2,1)S(1)}, bf16[8,64,768]{2,1,0:T(8,128)(2,1)S(1)}, u32[]{:S(2)}, u32[]{:S(2)}) %collective-permute-start.1) | collective-permute-done | bytes 786464 | tf_op jit(solution)/shard_map/ppermute | solution.py:54
  97.7 3.6 collective-permute-start.2
  112.8 6.2 collective-permute-done.2
  123.8 478.8 %all-to-all-done.1 = bf16[128,1,64,768]{3,2,1,0:T(8,128)(2,1)} async-done(((bf16[128,1,64,768]{3,2,1,0:T(8,128)(2,1)}), bf16[128,1,64,768]{3,2,1,0:T(8,128)(2,1)}, u32[]{:S(2)}, u32[]{:S(2)}) %all-to-all-start.1) | async-done | bytes 12582944 | tf_op jit(solution)/shard_map/all_to_all | solution.py:77
  602.6 242.0 %while.10 = (s32[]{:T(128)}, bf16[8,64,384]{2,1,0:T(8,128)(2,1)}, s32[8,4]{1,0:T(8,128)}, bf16[32,64,768]{2,1,0:T(8,128)(2,1)}, s32[8,16]{1,0:T(8,128)S(1)}, /*i...) while((s32[]{:T(128)}, bf16[8,64,384]{2,1,0:T(8,128)(2,1)}, ...), condition=%wide.region_8.9_spmd, body=%wide.region_5.8_spmd.sunk | while | flops 132760128 | bytes 37876240 | solution.py:87
  608.4 5.2 gather_fusion.1
  614.9 3.0 fusion.76
  638.6 5.2 gather_fusion.1
  645.1 3.0 fusion.76
  668.9 5.2 gather_fusion.1
  675.4 3.0 fusion.76
  699.1 5.2 gather_fusion.1
  729.4 5.2 gather_fusion.1
  759.6 5.2 gather_fusion.1
  789.9 5.2 gather_fusion.1
  820.1 5.2 gather_fusion.1
  846.4 3.5 fusion.29
  (239 shorter events, 221.0 us)
Async XLA Ops:
  0.0 846.3 %copy-start = (bf16[1536,384]{1,0:T(8,128)(2,1)S(1)}, bf16[1536,384]{1,0:T(8,128)(2,1)}, u32[]{:S(2)}) copy-start(bf16[1536,384]{1,0:T(8,128)(2,1)} %param.19) | copy-start | bytes 3538948
  1.6 0.9 copy-start.4
  2.9 0.9 copy-start.5
  3.8 33.5 %all-to-all-start = ((s32[128,1,1]{2,1,0:T(1,128)}), s32[128,1,1]{2,1,0:T(1,128)S(1)}, u32[]{:S(2)}, u32[]{:S(2)}) async-start(s32[128,1,1]{2,1,0:T(1,128)} %copy.48), calls=%async_computation | async-start | bytes 131072 | tf_op jit(solution)/shard_map/all_to_all | solution.py:73
  24.2 0.8 copy-start.2
  27.1 1.1 copy-start.3
  48.0 554.7 %all-to-all-start.1 = ((bf16[128,1,64,768]{3,2,1,0:T(8,128)(2,1)}), bf16[128,1,64,768]{3,2,1,0:T(8,128)(2,1)}, u32[]{:S(2)}, u32[]{:S(2)}) async-start(bf16[128,1,64,768]{3,2,1,0:T(8,128)(2,1)} %bitcast.77), calls=%async_computation.1 | async-start | bytes 25165824 | tf_op jit(solution)/shard_map/all_to_all | solution.py:77
  55.5 21.5 %collective-permute-start = (bf16[8,64,768]{2,1,0:T(8,128)(2,1)S(1)}, bf16[8,64,768]{2,1,0:T(8,128)(2,1)S(1)}, u32[]{:S(2)}, u32[]{:S(2)}) collective-permute-start(bf16[8,64,768]{2,1,0:T(8,128)(2,1)S(1)} %bitcast.74), channel_id=1, source_target_pairs={{0,1},{1,2},{2,3},{3,0},{4,5},{5,6},{6,7},{7,4},{8,9},{9,10},{10,1... | collective-permute-start | bytes 2359304 | tf_op jit(solution)/shard_map/ppermute | solution.py:54
  76.9 20.8 %collective-permute-start.1 = (bf16[8,64,768]{2,1,0:T(8,128)(2,1)S(1)}, bf16[8,64,768]{2,1,0:T(8,128)(2,1)S(1)}, u32[]{:S(2)}, u32[]{:S(2)}) collective-permute-start(bf16[8,64,768]{2,1,0:T(8,128)(2,1)S(1)} %collective-permute-done), channel_id=1, source_target_pairs={{0,1},{1,2},{2,3},{3,0},{4,5},{5,6},{6,7},{7,4},{8,9},{9,10},{10,1... | collective-permute-start | bytes 2359304 | tf_op jit(solution)/shard_map/ppermute | solution.py:54
  97.7 21.2 %collective-permute-start.2 = (bf16[8,64,768]{2,1,0:T(8,128)(2,1)S(1)}, bf16[8,64,768]{2,1,0:T(8,128)(2,1)}, u32[]{:S(2)}, u32[]{:S(2)}) collective-permute-start(bf16[8,64,768]{2,1,0:T(8,128)(2,1)S(1)} %collective-permute-done.1), channel_id=1, source_target_pairs={{0,1},{1,2},{2,3},{3,0},{4,5},{5,6},{6,7},{7,4},{8,9},{9,10},{10,1... | collective-permute-start | bytes 2359304 | tf_op jit(solution)/shard_map/ppermute | solution.py:54
  121.7 480.9 %copy-start.6 = (pred[8,20]{1,0:T(8,128)(4,1)S(1)}, pred[8,20]{1,0:T(8,128)(4,1)}, u32[]{:S(2)}) copy-start(pred[8,20]{1,0:T(8,128)(4,1)} %copy.51) | copy-start | bytes 484
  602.6 243.7 %copy-start.7 = (f32[384]{0:T(512)S(1)}, f32[384]{0:T(512)}, u32[]{:S(2)}) copy-start(f32[384]{0:T(512)} %param.17) | copy-start | bytes 4612
  630.2 1.2 copy-start.1
  660.5 1.2 copy-start.1
  690.7 1.2 copy-start.1
  721.0 1.2 copy-start.1
  751.3 1.2 copy-start.1
  781.5 1.2 copy-start.1
  811.8 1.2 copy-start.1
  842.0 1.2 copy-start.1
